TPU v7x, 32 devices: a whole 2x2x4 slice. The times are simulated.
32 devices in a mesh: groups: 2 (over y), row: 16 (over z, x, core).
Axes of the slice: x: 2, y: 2, z: 4, core: 2. Of those that a mesh axis runs over, the one named last changes fastest.
Arguments:
- activations: bfloat16 [768, 8192], P('groups', 'row'), parts along dimension 0, may hold values from -24 to 24
- norm_gain: bfloat16 [8192], P('row'), may hold values from 0.099609375 to 1.8984375
- gate_weight: bfloat16 [8192, 28672], P(None, 'row'), may hold values from -0.0625 to 0.0625
- up_weight: bfloat16 [8192, 28672], P(None, 'row'), may hold values from -0.0625 to 0.0625
- down_weight: bfloat16 [28672, 8192], P('row'), may hold values from -0.046875 to 0.046875
Outputs:
- mlp_out: bfloat16 [768, 8192], P('groups', 'row'), parts along dimension 0
There are 2 independent parts, one for each index of `groups`. A program takes and returns all parts, laid end to end along the dimension named above; an argument that names none is the same for every part. Nothing has to cross between parts.
All inputs are finite; a program needn't handle non-finite values.
Results may differ from a plain program's by a relative error of at most 0.0065.
Values may be sent and summed in bfloat16 or wider, within the bound.
A program may use at most 192 MiB of HBM per device.

v0:
```python
import jax
import jax.numpy as jnp
from jax import lax
from jax.sharding import PartitionSpec as P

D = 8192


def per_device(activations, norm_gain, gate_weight, up_weight, down_weight):
    float_rows = activations.astype(jnp.float32)
    square_sums = lax.psum(jnp.sum(float_rows * float_rows, axis=1), "row")
    inv_scale = lax.rsqrt(square_sums / D + 1e-05)
    normed = (float_rows * inv_scale[:, None] * norm_gain.astype(jnp.float32)[None, :]).astype(
        jnp.bfloat16
    )
    shard_rows = lax.all_gather(normed, "row", axis=1, tiled=True)
    gate_proj = jnp.dot(shard_rows, gate_weight, preferred_element_type=jnp.float32)
    up_proj = jnp.dot(shard_rows, up_weight, preferred_element_type=jnp.float32)
    hidden = (jax.nn.silu(gate_proj) * up_proj).astype(jnp.bfloat16)
    reduced = lax.psum_scatter(
        lax.dot_general(
            down_weight, hidden, (((0,), (1,)), ((), ())), preferred_element_type=jnp.float32
        ),
        "row",
        scatter_dimension=0,
        tiled=True,
    )
    return reduced.T.astype(jnp.bfloat16)


def solution(mesh):
    in_specs = (P("groups", "row"), P("row"), P(None, "row"), P(None, "row"), P("row", None))
    out_specs = P("groups", "row")
    return jax.shard_map(
        per_device, mesh=mesh, in_specs=in_specs, out_specs=out_specs, check_vma=False
    )
```

profile of v0, /device:TPU:0, one launch (start us, length us, event | category | flops | bytes accessed | tf_op | source)
XLA Modules:
  0.0 305.9 jit_solution(5603079134771323414)
XLA Ops:
  6.5 0.0 all-gather.2.cloned.1.call-start
  6.5 0.7 convert_element_type.19
  7.2 1.2 fusion.1
  8.4 34.9 %psum.7 = f32[384]{0:T(512)S(1)} all-reduce(f32[384]{0:T(512)S(1)} %fusion.1), channel_id=1, replica_groups=mesh['groups'=2,'row'=16] {'row'}, use_global_device_ids=true, to_apply=%region_1.0 | all-reduce | flops 384 | bytes 3072 | tf_op jit(solution)/shard_map/psum | solution.py:11
  43.3 1.9 fusion.3
  45.2 0.0 all-gather.2.cloned.1.call-update
  45.2 0.0 reduce-scatter.2.cloned.1.call-start
  45.3 62.6 %all-gather.2.cloned.1.call-done = bf16[384,8192]{1,0:T(8,128)(2,1)} async-done(((bf16[384,512]{1,0:T(8,128)(2,1)}), bf16[384,8192]{1,0:T(8,128)(2,1)}) %all-gather.2.cloned.1.call-update) | async-done | bytes 6291472 | tf_op jit(solution)/shard_map/all_gather | solution.py:16
  107.9 0.0 copy-start
  107.9 19.6 %fusion.4 = f32[384,1792]{1,0:T(8,128)} fusion(bf16[384,8192]{1,0:T(8,128)(2,1)} %all-gather.2.cloned.1.call-done, bf16[8192,1792]{1,0:T(8,128)(2,1)} %param.7), kind=kOutput, calls=%fused_computation.10 | convolution fusion | flops 11274289152 | bytes 38404096 | tf_op jit(solution)/shard_map/dot_general | solution.py:17
  127.5 0.0 copy-done
  127.5 16.7 %fusion = bf16[384,1792]{1,0:T(8,128)(2,1)S(1)} fusion(bf16[384,8192]{1,0:T(8,128)(2,1)S(1)} %copy-done, bf16[8192,1792]{1,0:T(8,128)(2,1)} %param.8, f32[384,1792]{1,0:T(8,128)} %fusion.4), kind=kOutput, calls=%fused_computation.2 | convolution fusion | flops 11278417920 | bytes 39780352 | tf_op jit(solution)/shard_map/dot_general | solution.py:18
  144.2 19.8 %convolution_bitcast_fusion = f32[8192,384]{0,1:T(8,128)} fusion(bf16[384,1792]{1,0:T(8,128)(2,1)S(1)} %fusion, bf16[1792,8192]{1,0:T(8,128)(2,1)} %param.9), kind=kOutput, calls=%fused_computation | convolution fusion | flops 11274289152 | bytes 43319296 | tf_op jit(solution)/shard_map/dot_general | solution.py:21
  164.0 0.0 reduce-scatter.2.cloned.1.call-update
  164.0 133.1 %reduce-scatter.2.cloned.1.call-done = f32[512,384]{0,1:T(8,128)} async-done(((f32[8192,384]{0,1:T(8,128)}), f32[512,384]{0,1:T(8,128)}) %reduce-scatter.2.cloned.1.call-update) | async-done | bytes 786448 | tf_op jit(solution)/shard_map/reduce_scatter | solution.py:20
  297.1 1.9 convert_bitcast_fusion
  (1 shorter events, 0.0 us)
Async XLA Ops:
  6.5 101.4 %all-gather.2.cloned.1.call-start = ((), (), s32[]{:S(2)}) async-start(), calls=%async_computation.1 | async-start | bytes 6684672 | tf_op jit(solution)/shard_map/all_gather | solution.py:16
  45.2 251.9 %reduce-scatter.2.cloned.1.call-start = ((), (), s32[]{:S(2)}) async-start(), calls=%async_computation.2 | async-start | bytes 13369344 | tf_op jit(solution)/shard_map/reduce_scatter | solution.py:20
  107.9 19.6 %copy-start = (bf16[384,8192]{1,0:T(8,128)(2,1)S(1)}, bf16[384,8192]{1,0:T(8,128)(2,1)}, u32[]{:S(2)}) copy-start(bf16[384,8192]{1,0:T(8,128)(2,1)} %all-gather.2.cloned.1.call-done) | copy-start | bytes 18874372
Sparse Core Ops, SparseCore 0:
  45.4 62.5 all-gather.1
  164.1 132.9 reduce-scatter.1
where the time goes:
time: 306 us
  waiting for transfers between devices  196 us (64%)
  matrix products  56.1 us (18%)
  blocking collectives  34.9 us (11%)
  between operations  13.4 us (4%)
  other arithmetic  5.67 us (2%)
    reduce_scatter x1, waiting for transfers between devices, per_device(): lax.psum_scatter(lax.dot_general(down_weight, hidden, (((0,), (1,)), ((),...  133 us
    all_gather x1, waiting for transfers between devices, per_device(): shard_rows = lax.all_gather(normed, 'row', axis=1, tiled=True)  62.6 us
    psum x1, blocking collectives, per_device(): square_sums = lax.psum(jnp.sum(float_rows * float_rows, axis=1), 'row')  34.9 us
    dot_general x1, matrix products, per_device(): lax.dot_general(down_weight, hidden, (((0,), (1,)), ((), ())), preferred_...  19.8 us
    dot_general x1, matrix products, per_device(): jnp.dot(shard_rows, gate_weight, preferred_element_type=jnp.float32)  19.6 us
    dot_general x1, matrix products, per_device(): up_proj = jnp.dot(shard_rows, up_weight, preferred_element_type=jnp.float32)  16.7 us
  transfers between devices with their start and end apart: 2, of which 2 were waited for; matrix products, arithmetic and copies ran while one was open for 0% of the time, Pallas kernels for 0%

commit v1 on v0

--- a/solution.py
+++ b/solution.py
@@ -2,13 +2,15 @@
 import jax.numpy as jnp
 from jax import lax
 from jax.sharding import PartitionSpec as P
+from jax.lax import all_gather
 
 D = 8192
 
 
 def per_device(activations, norm_gain, gate_weight, up_weight, down_weight):
     float_rows = activations.astype(jnp.float32)
-    square_sums = lax.psum(jnp.sum(float_rows * float_rows, axis=1), "row")
+    _put_copies = lambda xx: jnp.sum(all_gather(xx, "row"), 0)
+    square_sums = _put_copies(jnp.sum(float_rows * float_rows, axis=1))
     inv_scale = lax.rsqrt(square_sums / D + 1e-05)
     normed = (float_rows * inv_scale[:, None] * norm_gain.astype(jnp.float32)[None, :]).astype(
         jnp.bfloat16

time: 306 us -> 295 us (0.964)
  blocking collectives: 34.9 us -> 23.2 us
    psum x1 -> x0, blocking collectives: 34.9 us -> none  [per_device(): square_sums = lax.psum(jnp.sum(float_rows * float_rows, axis=1), 'row')]
    all_gather x0 -> x1, blocking collectives: none -> 23.2 us  [per_device(): _put_copies = lambda xx: jnp.sum(all_gather(xx, 'row'), 0)]
where the time goes in v1:
time: 295 us; the launch traced here: 294 us
  waiting for transfers between devices  196 us (66%)
  matrix products  56.1 us (19%)
  blocking collectives  23.2 us (8%)
  between operations  13.4 us (5%)
  other arithmetic  5.71 us (2%)
    reduce_scatter x1, waiting for transfers between devices, per_device(): lax.psum_scatter(lax.dot_general(down_weight, hidden, (((0,), (1,)), ((),...  133 us
    all_gather x1, waiting for transfers between devices, per_device(): shard_rows = lax.all_gather(normed, 'row', axis=1, tiled=True)  62.6 us
    all_gather x1, blocking collectives, per_device(): _put_copies = lambda xx: jnp.sum(all_gather(xx, 'row'), 0)  23.2 us
    dot_general x1, matrix products, per_device(): lax.dot_general(down_weight, hidden, (((0,), (1,)), ((), ())), preferred_...  19.8 us
    dot_general x1, matrix products, per_device(): jnp.dot(shard_rows, gate_weight, preferred_element_type=jnp.float32)  19.5 us
    dot_general x1, matrix products, per_device(): up_proj = jnp.dot(shard_rows, up_weight, preferred_element_type=jnp.float32)  16.7 us
  transfers between devices with their start and end apart: 2, of which 2 were waited for; matrix products, arithmetic and copies ran while one was open for 0% of the time, Pallas kernels for 0%

profile of v1, /device:TPU:0, one launch (start us, length us, event | category | flops | bytes accessed | tf_op | source)
XLA Modules:
  0.0 294.2 jit_solution(5311400101785194598)
XLA Ops:
  6.5 0.0 all-gather.4.cloned.1.call-start
  6.5 0.7 convert_element_type.19
  7.2 1.2 fusion.1
  8.4 23.2 %all-gather.1 = f32[16,1,384]{2,1,0:T(1,128)S(1)} all-gather(f32[1,1,384]{2,1,0:T(1,128)S(1)} %reshape.7), channel_id=2, replica_groups=mesh['groups'=2,'row'=16] {'row'}, dimensions={0}, use_global_device_ids=true | all-gather | bytes 26112 | tf_op jit(solution)/shard_map/all_gather | solution.py:12
  31.6 1.9 fusion.3
  33.5 0.0 all-gather.4.cloned.1.call-update
  33.5 0.0 reduce-scatter.2.cloned.1.call-start
  33.6 62.6 %all-gather.4.cloned.1.call-done = bf16[384,8192]{1,0:T(8,128)(2,1)} async-done(((bf16[384,512]{1,0:T(8,128)(2,1)}), bf16[384,8192]{1,0:T(8,128)(2,1)}) %all-gather.4.cloned.1.call-update) | async-done | bytes 6291472 | tf_op jit(solution)/shard_map/all_gather | solution.py:18
  96.2 0.0 copy-start
  96.2 19.5 %fusion.4 = f32[384,1792]{1,0:T(8,128)} fusion(bf16[384,8192]{1,0:T(8,128)(2,1)} %all-gather.4.cloned.1.call-done, bf16[8192,1792]{1,0:T(8,128)(2,1)} %param.7), kind=kOutput, calls=%fused_computation.10 | convolution fusion | flops 11274289152 | bytes 38404096 | tf_op jit(solution)/shard_map/dot_general | solution.py:19
  115.8 0.0 copy-done
  115.8 16.7 %fusion = bf16[384,1792]{1,0:T(8,128)(2,1)S(1)} fusion(bf16[384,8192]{1,0:T(8,128)(2,1)S(1)} %copy-done, bf16[8192,1792]{1,0:T(8,128)(2,1)} %param.8, f32[384,1792]{1,0:T(8,128)} %fusion.4), kind=kOutput, calls=%fused_computation.2 | convolution fusion | flops 11278417920 | bytes 39780352 | tf_op jit(solution)/shard_map/dot_general | solution.py:20
  132.5 19.8 %convolution_bitcast_fusion = f32[8192,384]{0,1:T(8,128)} fusion(bf16[384,1792]{1,0:T(8,128)(2,1)S(1)} %fusion, bf16[1792,8192]{1,0:T(8,128)(2,1)} %param.9), kind=kOutput, calls=%fused_computation | convolution fusion | flops 11274289152 | bytes 43319296 | tf_op jit(solution)/shard_map/dot_general | solution.py:23
  152.3 0.0 reduce-scatter.2.cloned.1.call-update
  152.3 133.1 %reduce-scatter.2.cloned.1.call-done = f32[512,384]{0,1:T(8,128)} async-done(((f32[8192,384]{0,1:T(8,128)}), f32[512,384]{0,1:T(8,128)}) %reduce-scatter.2.cloned.1.call-update) | async-done | bytes 786448 | tf_op jit(solution)/shard_map/reduce_scatter | solution.py:22
  285.4 1.9 convert_bitcast_fusion
  (3 shorter events, 0.1 us)
Async XLA Ops:
  6.5 89.7 %all-gather.4.cloned.1.call-start = ((), (), s32[]{:S(2)}) async-start(), calls=%async_computation.1 | async-start | bytes 6684672 | tf_op jit(solution)/shard_map/all_gather | solution.py:18
  33.5 251.9 %reduce-scatter.2.cloned.1.call-start = ((), (), s32[]{:S(2)}) async-start(), calls=%async_computation.2 | async-start | bytes 13369344 | tf_op jit(solution)/shard_map/reduce_scatter | solution.py:22
  96.2 19.6 %copy-start = (bf16[384,8192]{1,0:T(8,128)(2,1)S(1)}, bf16[384,8192]{1,0:T(8,128)(2,1)}, u32[]{:S(2)}) copy-start(bf16[384,8192]{1,0:T(8,128)(2,1)} %all-gather.4.cloned.1.call-done) | copy-start | bytes 18874372
Sparse Core Ops, SparseCore 0:
  33.6 62.5 all-gather.3
  152.4 132.9 reduce-scatter.1
